TPU v7x, 32 devices: a whole 2x2x4 slice. The times are simulated.
32 devices in a mesh: seq: 16 (over z, y, x), head: 2 (over core).
Axes of the slice: x: 2, y: 2, z: 4, core: 2. Of those that a mesh axis runs over, the one named last changes fastest.
Arguments:
- raw_keys: bfloat16 [2, 16384, 8, 128], P(None, 'seq', 'head'), may hold values from -6 to 6
- raw_values: bfloat16 [2, 16384, 8, 128], P(None, 'seq', 'head'), may hold values from -6 to 6
- phase: int32 [2], replicated, may hold values from 0 to 255, as said below
- ratio: int32 [2, 16], replicated, may hold values from 8 to 32, as said below
- resident_len: int32 [2, 16], replicated, may hold values from 1 to 256, as said below
- beacon_queries: bfloat16 [2, 2048, 8, 8, 128], P(None, 'seq', 'head'), may hold values from -150 to 150
- beacon_wk: bfloat16 [8192, 1024], P('seq', 'head'), may hold values from -0.125 to 0.125
- beacon_wv: bfloat16 [8192, 1024], P('seq', 'head'), may hold values from -0.125 to 0.125
- resident_keys: bfloat16 [2, 4096, 8, 128], P(None, 'seq', 'head'), may hold values from -6 to 6
- resident_values: bfloat16 [2, 4096, 8, 128], P(None, 'seq', 'head'), may hold values from -6 to 6
- decode_queries: bfloat16 [4, 2, 8, 8, 128], P(None, None, 'head'), may hold values from -150 to 150
- out_weight: bfloat16 [8192, 8192], P('head', 'seq'), may hold values from -0.0625 to 0.0625
Outputs:
- beacon_keys: bfloat16 [2, 2048, 8, 128], P(None, 'seq', 'head')
- beacon_values: bfloat16 [2, 2048, 8, 128], P(None, 'seq', 'head')
- projected: bfloat16 [4, 2, 8192], P(None, None, 'seq')
Inputs may be any that keep to these rules, and one draw needn't show every extreme that they name: `phase`: some request has 255. `ratio`: each value is 1024 // 128 times 1, 2 or 4; both ends occur. `resident_len`: some pair has 256.
All inputs are finite; a program needn't handle non-finite values.
Results may differ from a plain program's by a relative error of at most 0.025.
Values may be sent and summed in bfloat16 or wider, within the bound.
A program may use at most 64 MiB of HBM per device.

v0:
```python
import math
import jax
import jax.numpy as jnp
from jax import lax
from jax.sharding import PartitionSpec as P

G = 8
INTERVAL = 1024
NB = 128
OFF = 256
STEPS = 4
masked_score = -1e30


def shifted(value, axis, steps):
    count = lax.axis_size(axis)
    first, last = (max(0, -steps), min(count, count - steps))
    return lax.ppermute(value, axis, [(source, source + steps) for source in range(first, last)])


def joined(shard, axis, combine):
    everything = jax.tree.map(lambda part: lax.all_gather(part, axis), shard)
    first = jax.tree.map(lambda part: part[0], everything)

    def hop(k, so_far):
        return combine(so_far, jax.tree.map(lambda part: part[k], everything))

    return lax.fori_loop(1, lax.axis_size(axis), hop, first)


def blend(former, latter):
    row_peak = jnp.maximum(former[0], latter[0])
    former_scale = jnp.exp(former[0] - row_peak)
    latter_scale = jnp.exp(latter[0] - row_peak)
    weight_sum = former[1] * former_scale + latter[1] * latter_scale
    weighted = former[2] * former_scale[..., None] + latter[2] * latter_scale[..., None]
    return (row_peak, weight_sum, weighted)


def pool_part(queries, key_rows, value_rows, positions, present, reaches):
    inv_root = 1.0 / math.sqrt(queries.shape[-1])

    def per_request(members):
        query_block, key_block, value_block, position_row, present_row, reach_row = members
        scores = (
            jnp.einsum("jkgd,ikd->jkgi", query_block, key_block, preferred_element_type=jnp.float32)
            * inv_root
        )
        allowed = (
            present_row[None, :]
            & (position_row[None, :] >= 0)
            & (position_row[None, :] < INTERVAL)
            & (position_row[None, :] < reach_row[:, None])
        )
        cache_mask = allowed[:, None, None, :]
        row_peak = jnp.max(jnp.where(cache_mask, scores, masked_score), axis=-1)
        weights = jnp.where(cache_mask, jnp.exp(scores - row_peak[..., None]), 0.0)
        weight_sum = jnp.sum(weights, axis=-1)
        weighted = jnp.einsum(
            "jkgi,ikd->jkgd",
            weights.astype(jnp.bfloat16),
            value_block,
            preferred_element_type=jnp.float32,
        )
        return (row_peak, weight_sum, weighted)

    return lax.map(per_request, (queries, key_rows, value_rows, positions, present, reaches))


def body(
    raw_keys,
    raw_values,
    phase,
    ratio,
    resident_len,
    beacon_queries,
    beacon_wk,
    beacon_wv,
    resident_keys,
    resident_values,
    decode_queries,
    out_weight,
):
    requests = raw_keys.shape[0]
    kv_local = raw_keys.shape[2]
    head_dim = raw_keys.shape[3]
    shard_index = lax.axis_index("seq")
    shard_count = lax.axis_size("seq")
    is_first = shard_index == 0
    is_last = shard_index == shard_count - 1
    own_ratio = lax.dynamic_index_in_dim(ratio, shard_index, 1, keepdims=False)
    slot_ids = jnp.arange(NB, dtype=jnp.int32)
    lead_in = jnp.where(is_first, phase, 0)
    reaches = (slot_ids[None, :] + 1) * own_ratio[:, None] + lead_in[:, None]
    tail_keys = raw_keys[:, INTERVAL - OFF :]
    tail_values = raw_values[:, INTERVAL - OFF :]
    own_positions = jnp.arange(INTERVAL, dtype=jnp.int32)[None, :] + phase[:, None]
    rim_ids = jnp.arange(OFF, dtype=jnp.int32)
    rim_positions = rim_ids[None, :] - OFF + phase[:, None]
    near_keys, near_values = shifted((tail_keys, tail_values), "seq", 1)
    key_rows = jnp.concatenate([near_keys, raw_keys], axis=1)
    value_rows = jnp.concatenate([near_values, raw_values], axis=1)
    positions = jnp.concatenate([rim_positions, own_positions], axis=1)
    present = jnp.logical_not(is_first) | (positions >= phase[:, None])
    pooled_parts = pool_part(beacon_queries, key_rows, value_rows, positions, present, reaches)
    pooled = (pooled_parts[2] / pooled_parts[1][..., None]).astype(jnp.bfloat16)
    pooled_flat = pooled.reshape(requests * NB, kv_local * G * head_dim)
    pooled_whole = lax.all_gather(pooled_flat, "head", axis=1, tiled=True)
    key_sum = jnp.dot(
        pooled_whole,
        lax.all_gather(beacon_wk, "seq", axis=0, tiled=True),
        preferred_element_type=jnp.float32,
    )
    value_sum = jnp.dot(
        pooled_whole,
        lax.all_gather(beacon_wv, "seq", axis=0, tiled=True),
        preferred_element_type=jnp.float32,
    )
    made_keys = key_sum
    made_values = value_sum
    made_keys = made_keys.reshape(requests, NB, kv_local, head_dim)
    made_values = made_values.reshape(requests, NB, kv_local, head_dim)
    slot_live = slot_ids[None, :] < (INTERVAL // own_ratio)[:, None]
    beacon_keys = jnp.where(slot_live[:, :, None, None], made_keys, 0.0).astype(jnp.bfloat16)
    beacon_values = jnp.where(slot_live[:, :, None, None], made_values, 0.0).astype(jnp.bfloat16)
    cache_keys = jnp.concatenate([resident_keys, beacon_keys, tail_keys], axis=1)
    cache_values = jnp.concatenate([resident_values, beacon_values, tail_values], axis=1)
    own_len = lax.dynamic_index_in_dim(resident_len, shard_index, 1, keepdims=False)
    resident_ok = jnp.arange(resident_keys.shape[1], dtype=jnp.int32)[None, :] < own_len[:, None]
    leftover_ok = (rim_ids[None, :] >= OFF - phase[:, None]) & is_last
    usable = jnp.concatenate([resident_ok, slot_live, leftover_ok], axis=1)
    inv_root = 1.0 / math.sqrt(head_dim)
    scores = (
        jnp.einsum(
            "srkgd,rikd->rksgi", decode_queries, cache_keys, preferred_element_type=jnp.float32
        )
        * inv_root
    )
    cache_mask = usable[:, None, None, None, :]
    row_peak = jnp.max(jnp.where(cache_mask, scores, masked_score), axis=-1)
    weights = jnp.where(cache_mask, jnp.exp(scores - row_peak[..., None]), 0.0)
    weight_sum = jnp.sum(weights, axis=-1)
    weighted = jnp.einsum(
        "rksgi,rikd->rksgd",
        weights.astype(jnp.bfloat16),
        cache_values,
        preferred_element_type=jnp.float32,
    )
    merged = joined((row_peak, weight_sum, weighted), "seq", blend)
    total_sum = merged[1]
    total_weighted = merged[2]
    attended = (total_weighted / total_sum[..., None]).astype(jnp.bfloat16)
    attended = jnp.transpose(attended, (2, 0, 1, 3, 4)).reshape(
        STEPS * requests, kv_local * G * head_dim
    )
    partial_value = jnp.dot(attended, out_weight, preferred_element_type=jnp.float32)
    summed = lax.psum(partial_value, "head")
    projected = summed.astype(jnp.bfloat16).reshape(STEPS, requests, out_weight.shape[1])
    return (beacon_keys, beacon_values, projected)


def solution(mesh):
    return jax.shard_map(
        body,
        mesh=mesh,
        in_specs=(
            P(None, "seq", "head", None),
            P(None, "seq", "head", None),
            P(),
            P(),
            P(),
            P(None, "seq", "head", None, None),
            P("seq", "head"),
            P("seq", "head"),
            P(None, "seq", "head", None),
            P(None, "seq", "head", None),
            P(None, None, "head", None, None),
            P("head", "seq"),
        ),
        out_specs=(
            P(None, "seq", "head", None),
            P(None, "seq", "head", None),
            P(None, None, "seq"),
        ),
        check_vma=False,
    )
```

profile of v0, /device:TPU:0, one launch (start us, length us, event | category | flops | bytes accessed | tf_op | source)
XLA Modules:
  0.0 473.2 jit_solution(14405717227986694837)
XLA Ops:
  10.1 4.9 %collective-permute-start = (bf16[2,256,4,128]{3,1,2,0:T(8,128)(2,1)}, bf16[2,256,4,128]{3,1,2,0:T(8,128)(2,1)S(1)}, u32[]{:S(2)}, u32[]{:S(2)}) collective-permute-start(bf16[2,256,4,128]{3,1,2,0:T(8,128)(2,1)} %slice.23), channel_id=1, source_target_pairs={{0,2},{2,4},{4,6},{6,8},{8,10},{10,12},{12,14},{14,16},{16,18},{18... | collective-permute-start | bytes 1572872 | tf_op jit(solution)/shard_map/ppermute | solution.py:18
  15.8 4.2 collective-permute-start.1
  20.1 4.4 copy.50
  25.0 12.6 %collective-permute-done.1 = bf16[2,256,4,128]{3,1,2,0:T(8,128)(2,1)} collective-permute-done((bf16[2,256,4,128]{3,1,2,0:T(8,128)(2,1)}, bf16[2,256,4,128]{3,1,2,0:T(8,128)(2,1)}, u32[]{:S(2)}, u32[]{:S(2)}) %collective-permute-start.1) | collective-permute-done | bytes 524320 | tf_op jit(solution)/shard_map/ppermute | solution.py:18
  38.9 3.2 pad_maximum_fusion.1
  43.8 51.0 %while.31 = (s32[]{:T(128)}, f32[2,128,4,8]{1,3,2,0:T(8,128)S(1)}, f32[2,128,4,8,128]{1,4,3,2,0:T(8,128)}, pred[2,1280]{1,0:T(4,128)(4,1)S(1)}, s32[2,1280]{1,0:...) while((s32[]{:T(128)}, f32[2,128,4,8]{1,3,2,0:T(8,128)S(1)}, ...), condition=%wide.region_3.4_spmd, body=%wide.region_0.3_spmd.sunk | while | flops 2716145920 | bytes 71183224 | solution.py:67
  46.2 4.2 convolution_multiply_fusion.2
  50.4 11.6 %fusion.66 = (f32[128,4,8]{0,2,1:T(8,128)S(1)}, bf16[128,4,8,1280]{0,3,2,1:T(8,128)(2,1)}) fusion(f32[4,1280,128,8]{2,1,3,0:T(8,128)S(1)} %convolution_multiply_fusion.2, pred[128,1280]{0,1:T(8,128)(4,1)S(1)} %compare_and_fusion.3), kind=kOutput, calls=%fused_computation.85.clone.1 | output fusion | flops 26215680 | bytes 31637504 | tf_op jit(solution)/shard_map/while/body/eval_jaxpr/sub | solution.py:57
  62.1 7.3 %bitcast_dynamic-update-slice_fusion.5 = f32[2,128,4,8,128]{1,4,3,2,0:T(8,128)} fusion(f32[2,128,4,8,128]{1,4,3,2,0:T(8,128)} %get-tuple-element.439, s32[]{:T(128)} %get-tuple-element.437, bf16[128,4,8,1280]{0,3,2,1:T(8,128)(2,1)} %get-tuple-element.415, bf16[2,1280,4,128]{1,3,2,0:T(8,128)(2,1)} %get-tuple-element.455), kind=kOutput, calls=%fused_computation.19.clone.1 | convolution fusion | flops 1342177280 | bytes 13894656 | tf_op jit(solution)/shard_map/while/body/eval_jaxpr/jkgi,ikd->jkgd/dot_general | solution.py:59
  71.7 4.2 convolution_multiply_fusion.2
  75.9 11.6 %fusion.66 = (f32[128,4,8]{0,2,1:T(8,128)S(1)}, bf16[128,4,8,1280]{0,3,2,1:T(8,128)(2,1)}) fusion(f32[4,1280,128,8]{2,1,3,0:T(8,128)S(1)} %convolution_multiply_fusion.2, pred[128,1280]{0,1:T(8,128)(4,1)S(1)} %compare_and_fusion.3), kind=kOutput, calls=%fused_computation.85.clone.1 | output fusion | flops 26215680 | bytes 31637504 | tf_op jit(solution)/shard_map/while/body/eval_jaxpr/sub | solution.py:57
  87.5 7.3 %bitcast_dynamic-update-slice_fusion.5 = f32[2,128,4,8,128]{1,4,3,2,0:T(8,128)} fusion(f32[2,128,4,8,128]{1,4,3,2,0:T(8,128)} %get-tuple-element.439, s32[]{:T(128)} %get-tuple-element.437, bf16[128,4,8,1280]{0,3,2,1:T(8,128)(2,1)} %get-tuple-element.415, bf16[2,1280,4,128]{1,3,2,0:T(8,128)(2,1)} %get-tuple-element.455), kind=kOutput, calls=%fused_computation.19.clone.1 | convolution fusion | flops 1342177280 | bytes 13894656 | tf_op jit(solution)/shard_map/while/body/eval_jaxpr/jkgi,ikd->jkgd/dot_general | solution.py:59
  97.6 3.0 copy.52
  100.6 4.3 reshape.105
  106.8 14.1 %all-gather.8.cloned.1.call-done = bf16[256,8192]{1,0:T(8,128)(2,1)} async-done(((bf16[256,4096]{1,0:T(8,128)(2,1)}), bf16[256,8192]{1,0:T(8,128)(2,1)}) %all-gather.8.cloned.1.call-update) | async-done | bytes 4194320 | tf_op jit(solution)/shard_map/all_gather | solution.py:108
  120.9 116.3 %all-gather.10.cloned.1.call-done = bf16[8192,512]{1,0:T(8,128)(2,1)} async-done(((bf16[512,512]{1,0:T(8,128)(2,1)}), bf16[8192,512]{1,0:T(8,128)(2,1)}) %all-gather.10.cloned.1.call-update) | async-done | bytes 8388624 | tf_op jit(solution)/shard_map/all_gather | solution.py:111
  237.2 7.0 %fusion.45 = bf16[256,512]{1,0:T(8,128)(2,1)S(1)} fusion(bf16[256,8192]{1,0:T(8,128)(2,1)} %all-gather.8.cloned.1.call-done, bf16[8192,512]{1,0:T(8,128)(2,1)} %all-gather.10.cloned.1.call-done), kind=kOutput, calls=%fused_computation.86 | convolution fusion | flops 2147483648 | bytes 12845056 | tf_op jit(solution)/shard_map/dot_general | solution.py:109
  244.3 106.2 %all-gather.12.cloned.1.call-done = bf16[8192,512]{1,0:T(8,128)(2,1)} async-done(((bf16[512,512]{1,0:T(8,128)(2,1)}), bf16[8192,512]{1,0:T(8,128)(2,1)}) %all-gather.12.cloned.1.call-update) | async-done | bytes 8388624 | tf_op jit(solution)/shard_map/all_gather | solution.py:116
  350.5 7.0 %fusion.46 = bf16[256,512]{1,0:T(8,128)(2,1)S(1)} fusion(bf16[256,8192]{1,0:T(8,128)(2,1)} %all-gather.8.cloned.1.call-done, bf16[8192,512]{1,0:T(8,128)(2,1)} %all-gather.12.cloned.1.call-done), kind=kOutput, calls=%fused_computation.87 | convolution fusion | flops 2147483648 | bytes 12845056 | tf_op jit(solution)/shard_map/dot_general | solution.py:114
  363.7 39.8 %all-gather.1 = f32[32,4,4,8]{3,2,1,0:T(4,128)S(1)} all-gather(f32[2,4,4,8]{3,2,1,0:T(4,128)S(1)} %bitcast_reduce_fusion), channel_id=3, replica_groups=mesh['seq'=16,'head'=2] {'seq'}, dimensions={0}, use_global_device_ids=true | all-gather | bytes 17408 | tf_op jit(solution)/shard_map/all_gather | solution.py:22
  403.5 38.1 %all-gather = f32[32,4,4,8]{3,2,1,0:T(4,128)S(1)} all-gather(f32[2,4,4,8]{3,2,1,0:T(4,128)S(1)} %get-tuple-element.312), channel_id=2, replica_groups=mesh['seq'=16,'head'=2] {'seq'}, dimensions={0}, use_global_device_ids=true | all-gather | bytes 17408 | tf_op jit(solution)/shard_map/all_gather | solution.py:22
  442.6 17.0 %while.32 = (s32[]{:T(128)}, f32[2,4,4,8]{3,2,1,0:T(4,128)S(1)}, f32[2,4,4,8]{3,2,1,0:T(4,128)S(1)}, f32[2,4,4,8,128]{4,3,2,1,0:T(8,128)S(1)}, f32[16,2,4,4,8]{4...) while((s32[]{:T(128)}, f32[2,4,4,8]{3,2,1,0:T(4,128)S(1)}, ...), condition=%wide.region_7.8_spmd, body=%wide.region_6.7_spmd.sunk | while | flops 99845 | bytes 403607 | solution.py:28
  459.8 2.8 fusion.47
  462.6 3.4 psum.7
  (104 shorter events, 41.2 us)
Async XLA Ops:
  7.2 350.6 %copy-start = (bf16[4,2,4,8,128]{4,3,2,1,0:T(8,128)(2,1)S(1)}, bf16[4,2,4,8,128]{4,3,2,1,0:T(8,128)(2,1)}, u32[]{:S(2)}) copy-start(bf16[4,2,4,8,128]{4,3,2,1,0:T(8,128)(2,1)} %param.26) | copy-start | bytes 196612
  7.2 7.8 %slice-start = ((bf16[2,1024,4,128]{3,2,1,0:T(4,128)(2,1)}), bf16[2,256,4,128]{3,2,1,0:T(4,128)(2,1)S(1)}, s32[]{:S(2)}) async-start(bf16[2,1024,4,128]{3,2,1,0:T(4,128)(2,1)} %param.17), calls=%async_computation.4 | async-start | bytes 1048576 | tf_op jit(solution)/shard_map/slice | solution.py:96
  7.2 12.8 %copy-start.3 = (s32[2]{0:T(128)S(1)}, s32[2]{0:T(128)}, u32[]{:S(2)}) copy-start(s32[2]{0:T(128)} %param.18) | copy-start | bytes 28
  7.2 113.7 %all-gather.8.cloned.1.call-start = ((), (), s32[]{:S(2)}) async-start(), calls=%async_computation | async-start | bytes 6291456 | tf_op jit(solution)/shard_map/all_gather | solution.py:108
  9.2 15.3 %copy-start.4 = (s32[2,16]{1,0:T(2,128)S(1)}, s32[2,16]{1,0:T(2,128)}, u32[]{:S(2)}) copy-start(s32[2,16]{1,0:T(2,128)} %param.19) | copy-start | bytes 388
  9.2 15.3 %copy-start.5 = (s32[2,16]{1,0:T(2,128)S(1)}, s32[2,16]{1,0:T(2,128)}, u32[]{:S(2)}) copy-start(s32[2,16]{1,0:T(2,128)} %param.20) | copy-start | bytes 388
  10.1 32.1 %collective-permute-start = (bf16[2,256,4,128]{3,1,2,0:T(8,128)(2,1)}, bf16[2,256,4,128]{3,1,2,0:T(8,128)(2,1)S(1)}, u32[]{:S(2)}, u32[]{:S(2)}) collective-permute-start(bf16[2,256,4,128]{3,1,2,0:T(8,128)(2,1)} %slice.23), channel_id=1, source_target_pairs={{0,2},{2,4},{4,6},{6,8},{8,10},{10,12},{12,14},{14,16},{16,18},{18... | collective-permute-start | bytes 1572872 | tf_op jit(solution)/shard_map/ppermute | solution.py:18
  15.8 21.8 %collective-permute-start.1 = (bf16[2,256,4,128]{3,1,2,0:T(8,128)(2,1)}, bf16[2,256,4,128]{3,1,2,0:T(8,128)(2,1)}, u32[]{:S(2)}, u32[]{:S(2)}) collective-permute-start(bf16[2,256,4,128]{3,1,2,0:T(8,128)(2,1)} %copy.67), channel_id=1, source_target_pairs={{0,2},{2,4},{4,6},{6,8},{8,10},{10,12},{12,14},{14,16},{16,18},{18... | collective-permute-start | bytes 1572872 | tf_op jit(solution)/shard_map/ppermute | solution.py:18
  100.6 5.8 %copy-start.1 = (bf16[2,256,4,128]{3,2,1,0:T(4,128)(2,1)S(1)}, bf16[2,256,4,128]{3,2,1,0:T(4,128)(2,1)}, u32[]{:S(2)}) copy-start(bf16[2,256,4,128]{3,2,1,0:T(4,128)(2,1)} %param.24) | copy-start | bytes 1572868
  100.6 5.9 %copy-start.2 = (bf16[2,256,4,128]{3,2,1,0:T(4,128)(2,1)S(1)}, bf16[2,256,4,128]{3,2,1,0:T(4,128)(2,1)}, u32[]{:S(2)}) copy-start(bf16[2,256,4,128]{3,2,1,0:T(4,128)(2,1)} %param.25) | copy-start | bytes 1572868
  104.9 132.3 %all-gather.10.cloned.1.call-start = ((), (), s32[]{:S(2)}) async-start(), calls=%async_computation.1 | async-start | bytes 8912896 | tf_op jit(solution)/shard_map/all_gather | solution.py:111
  105.6 244.9 %all-gather.12.cloned.1.call-start = ((), (), s32[]{:S(2)}) async-start(), calls=%async_computation.2 | async-start | bytes 8912896 | tf_op jit(solution)/shard_map/all_gather | solution.py:116
  106.4 335.3 %all-gather.14.cloned.1.call-start = ((), (), s32[]{:S(2)}) async-start(), calls=%async_computation.3 | async-start | bytes 2228224 | tf_op jit(solution)/shard_map/all_gather | solution.py:22
Sparse Core Ops, SparseCore 0:
  105.0 15.8 all-gather.7
  123.7 113.4 all-gather.9
  240.0 110.4 all-gather.11
  361.7 60.6 all-gather.13
where the time goes:
time: 474 us; the launch traced here: 473 us
  waiting for transfers between devices  250 us (53%)
  blocking collectives  81.3 us (17%)
  other arithmetic  51.1 us (11%)
  matrix products  43.6 us (9%)
  local copies, waits for them, and re-layouts  22.9 us (5%)
  between operations  14 us (3%)
  starting transfers between devices  9.39 us (2%)
    all_gather x1, waiting for transfers between devices, body(): lax.all_gather(beacon_wk, 'seq', axis=0, tiled=True)  116 us
    all_gather x1, waiting for transfers between devices, body(): lax.all_gather(beacon_wv, 'seq', axis=0, tiled=True)  106 us
    all_gather x2, blocking collectives, joined(): everything = jax.tree.map(lambda part: lax.all_gather(part, axis), shard)  78 us
    sub x2, other arithmetic, per_request(): weights = jnp.where(cache_mask, jnp.exp(scores - row_peak[..., None]), 0.0)  23.3 us
    add x15, other arithmetic, blend(): former[2] * former_scale[..., None] + latter[2] * latter_scale[..., None]  16.1 us
    dot_general x2, matrix products, per_request(): jnp.einsum('jkgi,ikd->jkgd', weights.astype(jnp.bfloat16), value_block, p...  14.5 us
    all_gather x1, waiting for transfers between devices, body(): pooled_whole = lax.all_gather(pooled_flat, 'head', axis=1, tiled=True)  14.1 us
    ppermute x2, waiting for transfers between devices, shifted(): lax.ppermute(value, axis, [(source, source + steps) for source in range(f...  12.6 us
  transfers between devices with their start and end apart: 6, of which 4 were waited for; matrix products, arithmetic and copies ran while one was open for 4% of the time, Pallas kernels for 0%

commit v1 on v0

--- a/solution.py
+++ b/solution.py
@@ -10,6 +10,11 @@
 OFF = 256
 STEPS = 4
 masked_score = -1e30
+
+
+def gather_over(value, axis, dim):
+    sent = jnp.stack([value] * lax.axis_size(axis))
+    return jnp.concatenate(lax.all_to_all(sent, axis, 0, 0), axis=dim)
 
 
 def shifted(value, axis, steps):
@@ -107,9 +112,7 @@
     pooled_flat = pooled.reshape(requests * NB, kv_local * G * head_dim)
     pooled_whole = lax.all_gather(pooled_flat, "head", axis=1, tiled=True)
     key_sum = jnp.dot(
-        pooled_whole,
-        lax.all_gather(beacon_wk, "seq", axis=0, tiled=True),
-        preferred_element_type=jnp.float32,
+        pooled_whole, gather_over(beacon_wk, "seq", 0), preferred_element_type=jnp.float32
     )
     value_sum = jnp.dot(
         pooled_whole,

time: 474 us -> 536 us (1.13)
  blocking collectives: 81.3 us -> 113 us
  local copies, waits for them, and re-layouts: 22.9 us -> 50.7 us
  starting transfers between devices: 9.39 us -> 17.2 us
  waiting for transfers between devices: 250 us -> 244 us
    all_to_all x0 -> x1, waiting for transfers between devices: none -> 185 us  [gather_over(): return jnp.concatenate(lax.all_to_all(sent, axis, 0, 0), axis=dim)]
    all_gather x1 -> x0, waiting for transfers between devices: 116 us -> none  [body(): lax.all_gather(beacon_wk, 'seq', axis=0, tiled=True)]
    all_gather x1, waiting for transfers between devices: 106 us -> 45.6 us  [body(): lax.all_gather(beacon_wv, 'seq', axis=0, tiled=True)]
    all_gather x2, blocking collectives: 78 us -> 109 us  [joined(): everything = jax.tree.map(lambda part: lax.all_gather(part, axis), shard)]
    all_gather x1, waiting for transfers between devices: 14.1 us -> 0.01 us  [body(): pooled_whole = lax.all_gather(pooled_flat, 'head', axis=1, tiled=True)]
    all_to_all x0 -> x1, local copies, waits for them, and re-layouts: none -> 12.3 us  [gather_over(): return jnp.concatenate(lax.all_to_all(sent, axis, 0, 0), axis=dim)]
    dot_general x0 -> x1, local copies, waits for them, and re-layouts: none -> 11.4 us  [body(): jnp.dot(pooled_whole, gather_over(beacon_wk, 'seq', 0), preferred_element...]
    all_to_all x0 -> x1, starting transfers between devices: none -> 8.04 us  [gather_over(): return jnp.concatenate(lax.all_to_all(sent, axis, 0, 0), axis=dim)]
  transfers between devices with their start and end apart: 6 -> 6, of which waited for: 4 -> 3; matrix products, arithmetic and copies ran while one was open for 4% -> 8% of each run, Pallas kernels for 0% -> 0%
where the time goes in v1:
time: 536 us; the launch traced here: 534 us
  waiting for transfers between devices  244 us (46%)
  blocking collectives  113 us (21%)
  other arithmetic  51 us (10%)
  local copies, waits for them, and re-layouts  50.7 us (9%)
  matrix products  43.6 us (8%)
  starting transfers between devices  17.2 us (3%)
  between operations  14 us (3%)
    all_to_all x1, waiting for transfers between devices, gather_over(): return jnp.concatenate(lax.all_to_all(sent, axis, 0, 0), axis=dim)  185 us
    all_gather x2, blocking collectives, joined(): everything = jax.tree.map(lambda part: lax.all_gather(part, axis), shard)  109 us
    all_gather x1, waiting for transfers between devices, body(): lax.all_gather(beacon_wv, 'seq', axis=0, tiled=True)  45.6 us
    sub x2, other arithmetic, per_request(): weights = jnp.where(cache_mask, jnp.exp(scores - row_peak[..., None]), 0.0)  23.3 us
    add x15, other arithmetic, blend(): former[2] * former_scale[..., None] + latter[2] * latter_scale[..., None]  16.1 us
    dot_general x2, matrix products, per_request(): jnp.einsum('jkgi,ikd->jkgd', weights.astype(jnp.bfloat16), value_block, p...  14.6 us
    ppermute x2, waiting for transfers between devices, shifted(): lax.ppermute(value, axis, [(source, source + steps) for source in range(f...  12.6 us
    all_to_all x1, local copies, waits for them, and re-layouts, gather_over(): return jnp.concatenate(lax.all_to_all(sent, axis, 0, 0), axis=dim)  12.3 us
  transfers between devices with their start and end apart: 6, of which 3 were waited for; matrix products, arithmetic and copies ran while one was open for 8% of the time, Pallas kernels for 0%

profile of v1, /device:TPU:0, one launch (start us, length us, event | category | flops | bytes accessed | tf_op | source)
XLA Modules:
  0.0 533.8 jit_solution(11767406764172127933)
XLA Ops:
  10.0 4.9 collective-permute-start
  15.8 4.2 collective-permute-start.1
  20.1 4.4 copy.65
  25.0 12.6 %collective-permute-done.1 = bf16[2,256,4,128]{3,1,2,0:T(8,128)(2,1)} collective-permute-done((bf16[2,256,4,128]{3,1,2,0:T(8,128)(2,1)}, bf16[2,256,4,128]{3,1,2,0:T(8,128)(2,1)}, u32[]{:S(2)}, u32[]{:S(2)}) %collective-permute-start.1) | collective-permute-done | bytes 524320 | tf_op jit(solution)/shard_map/ppermute | solution.py:23
  43.8 51.0 %while.31 = (s32[]{:T(128)}, f32[2,128,4,8]{1,3,2,0:T(8,128)S(1)}, f32[2,128,4,8,128]{1,4,3,2,0:T(8,128)}, pred[2,1280]{1,0:T(4,128)(4,1)S(1)}, s32[2,1280]{1,0:...) while((s32[]{:T(128)}, f32[2,128,4,8]{1,3,2,0:T(8,128)S(1)}, ...), condition=%wide.region_3.4_spmd, body=%wide.region_0.3_spmd.sunk | while | flops 2716145920 | bytes 71183224 | solution.py:72
  46.2 4.2 convolution_multiply_fusion.2
  50.4 11.6 %fusion.65 = (f32[128,4,8]{0,2,1:T(8,128)S(1)}, bf16[128,4,8,1280]{0,3,2,1:T(8,128)(2,1)}) fusion(f32[4,1280,128,8]{2,1,3,0:T(8,128)S(1)} %convolution_multiply_fusion.2, pred[128,1280]{0,1:T(8,128)(4,1)S(1)} %compare_and_fusion.3), kind=kOutput, calls=%fused_computation.85.clone.1 | output fusion | flops 26215680 | bytes 31637504 | tf_op jit(solution)/shard_map/while/body/eval_jaxpr/sub | solution.py:62
  62.1 7.2 %bitcast_dynamic-update-slice_fusion.5 = f32[2,128,4,8,128]{1,4,3,2,0:T(8,128)} fusion(f32[2,128,4,8,128]{1,4,3,2,0:T(8,128)} %get-tuple-element.449, s32[]{:T(128)} %get-tuple-element.447, bf16[128,4,8,1280]{0,3,2,1:T(8,128)(2,1)} %get-tuple-element.425, bf16[2,1280,4,128]{1,3,2,0:T(8,128)(2,1)} %get-tuple-element.465), kind=kOutput, calls=%fused_computation.19.clone.1 | convolution fusion | flops 1342177280 | bytes 13894656 | tf_op jit(solution)/shard_map/while/body/eval_jaxpr/jkgi,ikd->jkgd/dot_general | solution.py:64
  71.6 4.2 convolution_multiply_fusion.2
  75.9 11.6 %fusion.65 = (f32[128,4,8]{0,2,1:T(8,128)S(1)}, bf16[128,4,8,1280]{0,3,2,1:T(8,128)(2,1)}) fusion(f32[4,1280,128,8]{2,1,3,0:T(8,128)S(1)} %convolution_multiply_fusion.2, pred[128,1280]{0,1:T(8,128)(4,1)S(1)} %compare_and_fusion.3), kind=kOutput, calls=%fused_computation.85.clone.1 | output fusion | flops 26215680 | bytes 31637504 | tf_op jit(solution)/shard_map/while/body/eval_jaxpr/sub | solution.py:62
  87.5 7.3 %bitcast_dynamic-update-slice_fusion.5 = f32[2,128,4,8,128]{1,4,3,2,0:T(8,128)} fusion(f32[2,128,4,8,128]{1,4,3,2,0:T(8,128)} %get-tuple-element.449, s32[]{:T(128)} %get-tuple-element.447, bf16[128,4,8,1280]{0,3,2,1:T(8,128)(2,1)} %get-tuple-element.425, bf16[2,1280,4,128]{1,3,2,0:T(8,128)(2,1)} %get-tuple-element.465), kind=kOutput, calls=%fused_computation.19.clone.1 | convolution fusion | flops 1342177280 | bytes 13894656 | tf_op jit(solution)/shard_map/while/body/eval_jaxpr/jkgi,ikd->jkgd/dot_general | solution.py:64
  100.6 4.2 reshape.110
  105.1 4.0 stack.2
  109.2 8.0 %all-to-all-start = ((bf16[16,512,512]{1,2,0:T(8,128)(2,1)}), bf16[16,512,512]{1,2,0:T(8,128)(2,1)}, u32[]{:S(2)}, u32[]{:S(2)}) async-start(bf16[16,512,512]{1,2,0:T(8,128)(2,1)} %stack.2), calls=%async_computation | async-start | bytes 16777216 | tf_op jit(solution)/shard_map/all_to_all | solution.py:17
  118.4 185.3 %all-to-all-done = bf16[16,512,512]{1,2,0:T(8,128)(2,1)} async-done(((bf16[16,512,512]{1,2,0:T(8,128)(2,1)}), bf16[16,512,512]{1,2,0:T(8,128)(2,1)}, u32[]{:S(2)}, u32[]{:S(2)}) %all-to-all-start) | async-done | bytes 8388640 | tf_op jit(solution)/shard_map/all_to_all | solution.py:17
  303.7 12.3 %copy.69 = bf16[16,512,512]{2,1,0:T(8,128)(2,1)} copy(bf16[16,512,512]{1,2,0:T(8,128)(2,1)} %all-to-all-done) | data formatting | bytes 16777216 | tf_op jit(solution)/shard_map/all_to_all | solution.py:17
  316.0 11.4 %copy.70 = bf16[512,8192]{1,0:T(8,128)(2,1)} copy(bf16[512,8192]{0,1:T(8,128)(2,1)} %bitcast.115) | data formatting | bytes 16777216 | tf_op jit(solution)/shard_map/dot_general | solution.py:114
  327.4 45.6 %all-gather.9.cloned.1.call-done = bf16[8192,512]{1,0:T(8,128)(2,1)} async-done(((bf16[512,512]{1,0:T(8,128)(2,1)}), bf16[8192,512]{1,0:T(8,128)(2,1)}) %all-gather.9.cloned.1.call-update) | async-done | bytes 8388624 | tf_op jit(solution)/shard_map/all_gather | solution.py:119
  372.9 7.0 %fusion.45 = bf16[256,512]{1,0:T(8,128)(2,1)S(1)} fusion(bf16[256,8192]{1,0:T(8,128)(2,1)} %all-gather.7.cloned.1.call-done, bf16[8192,512]{1,0:T(8,128)(2,1)} %all-gather.9.cloned.1.call-done), kind=kOutput, calls=%fused_computation.86 | convolution fusion | flops 2147483648 | bytes 12845056 | tf_op jit(solution)/shard_map/dot_general | solution.py:117
  380.1 7.0 %fusion.32 = bf16[2,128,4,128]{3,1,2,0:T(8,128)(2,1)S(1)} fusion(bf16[2,128,8192,1]{2,1,3,0:T(8,128)(2,1)} %bitcast.120, bf16[4,128,8192,1]{2,1,0,3:T(8,128)(2,1)} %bitcast.116, pred[2,128]{1,0:T(4,128)(4,1)S(1)} %iota_compare_fusion.1), kind=kOutput, calls=%fused_computation.52 | convolution fusion | flops 2147745792 | bytes 12845312 | tf_op jit(solution)/shard_map/dot_general | solution.py:114
  393.1 71.1 %all-gather.1 = f32[32,4,4,8]{3,2,1,0:T(4,128)S(1)} all-gather(f32[2,4,4,8]{3,2,1,0:T(4,128)S(1)} %bitcast_reduce_fusion), channel_id=3, replica_groups=mesh['seq'=16,'head'=2] {'seq'}, dimensions={0}, use_global_device_ids=true | all-gather | bytes 17408 | tf_op jit(solution)/shard_map/all_gather | solution.py:27
  464.2 38.2 %all-gather = f32[32,4,4,8]{3,2,1,0:T(4,128)S(1)} all-gather(f32[2,4,4,8]{3,2,1,0:T(4,128)S(1)} %get-tuple-element.322), channel_id=2, replica_groups=mesh['seq'=16,'head'=2] {'seq'}, dimensions={0}, use_global_device_ids=true | all-gather | bytes 17408 | tf_op jit(solution)/shard_map/all_gather | solution.py:27
  503.3 17.0 %while.32 = (s32[]{:T(128)}, f32[2,4,4,8]{3,2,1,0:T(4,128)S(1)}, f32[2,4,4,8]{3,2,1,0:T(4,128)S(1)}, f32[2,4,4,8,128]{4,3,2,1,0:T(8,128)S(1)}, f32[16,2,4,4,8]{4...) while((s32[]{:T(128)}, f32[2,4,4,8]{3,2,1,0:T(4,128)S(1)}, ...), condition=%wide.region_7.8_spmd, body=%wide.region_6.7_spmd.sunk | while | flops 99845 | bytes 403607 | solution.py:33
  523.3 3.4 psum.7
  (108 shorter events, 49.6 us)
Async XLA Ops:
  7.2 380.0 %copy-start = (bf16[4,2,4,8,128]{4,3,2,1,0:T(8,128)(2,1)S(1)}, bf16[4,2,4,8,128]{4,3,2,1,0:T(8,128)(2,1)}, u32[]{:S(2)}) copy-start(bf16[4,2,4,8,128]{4,3,2,1,0:T(8,128)(2,1)} %param.26) | copy-start | bytes 196612
  7.2 7.8 %slice-start = ((bf16[2,1024,4,128]{3,2,1,0:T(4,128)(2,1)}), bf16[2,256,4,128]{3,2,1,0:T(4,128)(2,1)S(1)}, s32[]{:S(2)}) async-start(bf16[2,1024,4,128]{3,2,1,0:T(4,128)(2,1)} %param.17), calls=%async_computation.4 | async-start | bytes 1048576 | tf_op jit(solution)/shard_map/slice | solution.py:101
  7.2 12.8 %copy-start.4 = (s32[2]{0:T(128)S(1)}, s32[2]{0:T(128)}, u32[]{:S(2)}) copy-start(s32[2]{0:T(128)} %param.18) | copy-start | bytes 28
  7.2 320.2 %all-gather.7.cloned.1.call-start = ((), (), s32[]{:S(2)}) async-start(), calls=%async_computation.1 | async-start | bytes 6291456 | tf_op jit(solution)/shard_map/all_gather | solution.py:113
  9.2 15.3 %copy-start.5 = (s32[2,16]{1,0:T(2,128)S(1)}, s32[2,16]{1,0:T(2,128)}, u32[]{:S(2)}) copy-start(s32[2,16]{1,0:T(2,128)} %param.19) | copy-start | bytes 388
  9.2 15.3 %copy-start.6 = (s32[2,16]{1,0:T(2,128)S(1)}, s32[2,16]{1,0:T(2,128)}, u32[]{:S(2)}) copy-start(s32[2,16]{1,0:T(2,128)} %param.20) | copy-start | bytes 388
  10.0 32.1 %collective-permute-start = (bf16[2,256,4,128]{3,1,2,0:T(8,128)(2,1)}, bf16[2,256,4,128]{3,1,2,0:T(8,128)(2,1)S(1)}, u32[]{:S(2)}, u32[]{:S(2)}) collective-permute-start(bf16[2,256,4,128]{3,1,2,0:T(8,128)(2,1)} %slice.23), channel_id=1, source_target_pairs={{0,2},{2,4},{4,6},{6,8},{8,10},{10,12},{12,14},{14,16},{16,18},{18... | collective-permute-start | bytes 1572872 | tf_op jit(solution)/shard_map/ppermute | solution.py:23
  15.8 21.8 %collective-permute-start.1 = (bf16[2,256,4,128]{3,1,2,0:T(8,128)(2,1)}, bf16[2,256,4,128]{3,1,2,0:T(8,128)(2,1)}, u32[]{:S(2)}, u32[]{:S(2)}) collective-permute-start(bf16[2,256,4,128]{3,1,2,0:T(8,128)(2,1)} %copy.85), channel_id=1, source_target_pairs={{0,2},{2,4},{4,6},{6,8},{8,10},{10,12},{12,14},{14,16},{16,18},{18... | collective-permute-start | bytes 1572872 | tf_op jit(solution)/shard_map/ppermute | solution.py:23
  100.6 4.3 copy-start.1
  109.2 8.9 %copy-start.2 = (bf16[2,256,4,128]{3,2,1,0:T(4,128)(2,1)S(1)}, bf16[2,256,4,128]{3,2,1,0:T(4,128)(2,1)}, u32[]{:S(2)}) copy-start(bf16[2,256,4,128]{3,2,1,0:T(4,128)(2,1)} %param.24) | copy-start | bytes 1572868
  109.2 8.9 %copy-start.3 = (bf16[2,256,4,128]{3,2,1,0:T(4,128)(2,1)S(1)}, bf16[2,256,4,128]{3,2,1,0:T(4,128)(2,1)}, u32[]{:S(2)}) copy-start(bf16[2,256,4,128]{3,2,1,0:T(4,128)(2,1)} %param.25) | copy-start | bytes 1572868
  109.2 194.6 %all-to-all-start = ((bf16[16,512,512]{1,2,0:T(8,128)(2,1)}), bf16[16,512,512]{1,2,0:T(8,128)(2,1)}, u32[]{:S(2)}, u32[]{:S(2)}) async-start(bf16[16,512,512]{1,2,0:T(8,128)(2,1)} %stack.2), calls=%async_computation | async-start | bytes 16777216 | tf_op jit(solution)/shard_map/all_to_all | solution.py:17
  117.2 255.7 %all-gather.9.cloned.1.call-start = ((), (), s32[]{:S(2)}) async-start(), calls=%async_computation.2 | async-start | bytes 8912896 | tf_op jit(solution)/shard_map/all_gather | solution.py:119
  118.0 384.4 %all-gather.11.cloned.1.call-start = ((), (), s32[]{:S(2)}) async-start(), calls=%async_computation.3 | async-start | bytes 2228224 | tf_op jit(solution)/shard_map/all_gather | solution.py:27
Sparse Core Ops, SparseCore 0:
  105.0 15.8 all-gather.6
  123.7 249.1 all-gather.8
  391.1 92.1 all-gather.10
